TPU v7x, 32 devices: a whole 2x2x4 slice. The times are simulated.
32 devices in a mesh: row: 2 (over x), col: 16 (over z, y, core).
Axes of the slice: x: 2, y: 2, z: 4, core: 2. Of those that a mesh axis runs over, the one named last changes fastest.
Arguments:
- activations: bfloat16 [128, 8192], P('col', 'row'), may hold values from -6 to 6
- up_weight: bfloat16 [8192, 53248], P('row', 'col'), may hold values from -0.0625 to 0.0625
- out_grad: bfloat16 [128, 53248], P('row', 'col'), may hold values from -6 to 6
- round_seed: int32 [1], replicated, may hold values from 0 to 1073741823
- counter_base: int32 [128], P('row'), may hold values from 0 to 1073741823
Outputs:
- weight_grad: float32 [8192, 53248], P('row', 'col')
- input_grad: bfloat16 [128, 8192], P('col', 'row')
All inputs are finite; a program needn't handle non-finite values.
Results may differ from a plain program's by a relative error of at most 0.015.
Values may be sent and summed in bfloat16 or wider, within the bound.
No kernel may reach another device: no remote copies, remote signals or barrier semaphores. Data moves between devices by JAX's collectives and lax.ppermute only.
A program may use at most 192 MiB of HBM per device.

v0:
```python
import jax
import jax.numpy as jnp
from jax import lax
from jax.sharding import PartitionSpec as P


def stochastic_round(grad, counter_base, round_seed, col_first):
    columns = col_first + lax.broadcasted_iota(jnp.int32, grad.shape, 1)
    counter = counter_base[:, None] + columns
    mixed = counter * jnp.int32(747796405) + round_seed[0] * jnp.int32(1013904223)
    mixed = mixed ^ mixed >> 15
    mixed = mixed * jnp.int32(277803737)
    mixed = mixed ^ mixed >> 16
    level = (mixed & 255).astype(jnp.float32)
    scaled = grad.astype(jnp.float32) * 4.0 + (level + 0.5) / 256.0
    return (jnp.floor(scaled) / 4.0).astype(jnp.bfloat16)


def contract(left, right):
    return lax.dot_general(
        left, right, (((0,), (0,)), ((), ())), preferred_element_type=jnp.float32
    )


def project(grad_rows, weight):
    return lax.dot_general(
        grad_rows, weight, (((1,), (1,)), ((), ())), preferred_element_type=jnp.float32
    )


def fold_panels(activations, combine, initial):
    everyone = lax.all_gather(activations, "col", axis=0, tiled=True)
    return combine(initial, everyone, 0)


def shards(activations, up_weight, out_grad, round_seed, counter_base):
    ff_local = out_grad.shape[1]
    d_local = activations.shape[1]
    col_first = lax.axis_index("col") * ff_local
    quantized = stochastic_round(out_grad, counter_base, round_seed, col_first)
    total_tokens = activations.shape[0] * lax.axis_size("col")
    scaling = total_tokens ** (-0.5)
    grad_zero = jnp.zeros((d_local, ff_local), jnp.float32)
    everything = lax.all_gather(quantized, "row", axis=0, tiled=True)

    def accumulate(total, panel, offset):
        return contract(panel, everything)

    weight_grad = fold_panels(activations, accumulate, grad_zero)
    input_grad = lax.psum_scatter(
        project(everything, up_weight).astype(jnp.bfloat16), "col", scatter_dimension=0, tiled=True
    )
    return (weight_grad * scaling, input_grad)


def solution(mesh):
    placed = (P("col", "row"), P("row", "col"), P("row", "col"), P(), P("row"))
    return jax.shard_map(
        shards,
        mesh=mesh,
        in_specs=placed,
        out_specs=(P("row", "col"), P("col", "row")),
        check_vma=False,
    )
```

profile of v0, /device:TPU:0, one launch (start us, length us, event | category | flops | bytes accessed | tf_op | source)
XLA Modules:
  0.0 130.5 jit_solution(6275972824914543225)
XLA Ops:
  7.2 0.0 all-gather.2.cloned.1.call-start
  7.2 0.7 all-gather.2.cloned.1.call-update
  7.9 0.0 reduce-scatter.2.cloned.1.call-start
  8.6 1.6 %fusion.8 = bf16[64,3328]{1,0:T(8,128)(2,1)S(1)} fusion(bf16[64,3328]{1,0:T(8,128)(2,1)} %param.7, s32[]{:T(128)} %bitcast, s32[3328]{0:T(1024)S(1)} %iota_add_fusion, s32[64]{0:T(128)} %param.9), kind=kLoop, calls=%fused_computation.12 | loop fusion | flops 3833856 | bytes 865540 | tf_op jit(solution)/shard_map/convert_element_type | solution.py:16
  10.2 13.5 %all_gather.6 = bf16[128,3328]{1,0:T(8,128)(2,1)S(1)} all-gather(bf16[64,3328]{1,0:T(8,128)(2,1)S(1)} %fusion.8), channel_id=1, replica_groups=mesh['row'=2,'col'=16] {'row'}, dimensions={0}, use_global_device_ids=true | all-gather | bytes 1277952 | tf_op jit(solution)/shard_map/all_gather | solution.py:44
  23.6 15.0 %convolution_convert_fusion = bf16[128,4096]{1,0:T(8,128)(2,1)} fusion(bf16[128,3328]{1,0:T(8,128)(2,1)S(1)} %all_gather.6, bf16[4096,3328]{1,0:T(8,128)(2,1)} %param.6), kind=kOutput, calls=%fused_computation.1 | convolution fusion | flops 3490185216 | bytes 29163520 | tf_op jit(solution)/shard_map/dot_general | solution.py:26
  38.6 0.0 reduce-scatter.2.cloned.1.call-update
  38.7 12.1 %all-gather.2.cloned.1.call-done = bf16[128,4096]{1,0:T(8,128)(2,1)} async-done(((bf16[8,4096]{1,0:T(8,128)(2,1)}), bf16[128,4096]{1,0:T(8,128)(2,1)}) %all-gather.2.cloned.1.call-update) | async-done | bytes 1048592 | tf_op jit(solution)/shard_map/all_gather | solution.py:32
  50.8 22.8 %multiply_bitcast_fusion = f32[4096,3328]{0,1:T(8,128)} fusion(bf16[128,3328]{1,0:T(8,128)(2,1)S(1)} %all_gather.6, bf16[128,4096]{1,0:T(8,128)(2,1)} %all-gather.2.cloned.1.call-done), kind=kOutput, calls=%fused_computation | convolution fusion | flops 3503292416 | bytes 56426496 | tf_op jit(solution)/shard_map/dot_general | solution.py:20
  73.6 50.1 %copy.7 = f32[4096,3328]{1,0:T(8,128)} copy(f32[4096,3328]{0,1:T(8,128)} %multiply_bitcast_fusion) | data formatting | bytes 109051904
  123.7 0.0 reduce-scatter.2.cloned.1.call-done
  (1 shorter events, 0.0 us)
Async XLA Ops:
  7.2 43.6 %all-gather.2.cloned.1.call-start = ((), (), s32[]{:S(2)}) async-start(), calls=%async_computation.1 | async-start | bytes 1114112 | tf_op jit(solution)/shard_map/all_gather | solution.py:32
  7.9 115.8 %reduce-scatter.2.cloned.1.call-start = ((), (), s32[]{:S(2)}) async-start(), calls=%async_computation.2 | async-start | bytes 1114112 | tf_op jit(solution)/shard_map/reduce_scatter | solution.py:50
Sparse Core Ops, SparseCore 0:
  10.1 40.5 all-gather.1
  54.9 56.5 reduce-scatter.1
where the time goes:
time: 131 us
  local copies, waits for them, and re-layouts  50.1 us (38%)
  matrix products  37.8 us (29%)
  between operations  14.7 us (11%)
  blocking collectives  13.5 us (10%)
  waiting for transfers between devices  12.8 us (10%)
  other arithmetic  1.56 us (1%)
    unnamed x1, local copies, waits for them, and re-layouts  50.1 us
    dot_general x1, matrix products, contract(): lax.dot_general(left, right, (((0,), (0,)), ((), ())), preferred_element_...  22.8 us
    dot_general x1, matrix products, project(): lax.dot_general(grad_rows, weight, (((1,), (1,)), ((), ())), preferred_el...  15 us
    all_gather x1, blocking collectives, shards(): everything = lax.all_gather(quantized, 'row', axis=0, tiled=True)  13.5 us
    all_gather x1, waiting for transfers between devices, fold_panels(): everyone = lax.all_gather(activations, 'col', axis=0, tiled=True)  12.1 us
  transfers between devices with their start and end apart: 2, of which 1 were waited for; matrix products, arithmetic and copies ran while one was open for 69% of the time, Pallas kernels for 0%

commit v1 on v0

--- a/solution.py
+++ b/solution.py
@@ -29,7 +29,9 @@
 
 
 def fold_panels(activations, combine, initial):
-    everyone = lax.all_gather(activations, "col", axis=0, tiled=True)
+    everyone = jnp.concatenate(
+        lax.all_to_all(jnp.stack([activations] * lax.axis_size("col")), "col", 0, 0), axis=0
+    )
     return combine(initial, everyone, 0)
 
 

time: 131 us -> 126 us (0.962)
  waiting for transfers between devices: 12.8 us -> 0.02 us
  starting transfers between devices: 0.08 us -> 7.46 us
  local copies, waits for them, and re-layouts: 50.1 us -> 52 us
    all_gather x1 -> x0, waiting for transfers between devices: 12.1 us -> none  [fold_panels(): everyone = lax.all_gather(activations, 'col', axis=0, tiled=True)]
    all_to_all x0 -> x1, starting transfers between devices: none -> 7.41 us  [fold_panels(): lax.all_to_all(jnp.stack([activations] * lax.axis_size('col')), 'col', 0, 0)]
    another operation x0 -> x1, local copies, waits for them, and re-layouts: none -> 1.91 us  [fold_panels(): jnp.stack([activations] * lax.axis_size('col'))]
  transfers between devices with their start and end apart: 2 -> 2, of which waited for: 1 -> 0; matrix products, arithmetic and copies ran while one was open for 69% -> 71% of each run, Pallas kernels for 0% -> 0%
where the time goes in v1:
time: 126 us; the launch traced here: 125 us
  local copies, waits for them, and re-layouts  52 us (41%)
  matrix products  36.6 us (29%)
  between operations  14.7 us (12%)
  blocking collectives  12.8 us (10%)
  starting transfers between devices  7.46 us (6%)
  other arithmetic  1.56 us (1%)
    unnamed x1, local copies, waits for them, and re-layouts  50.1 us
    dot_general x1, matrix products, contract(): lax.dot_general(left, right, (((0,), (0,)), ((), ())), preferred_element_...  21.6 us
    dot_general x1, matrix products, project(): lax.dot_general(grad_rows, weight, (((1,), (1,)), ((), ())), preferred_el...  15 us
    all_gather x1, blocking collectives, shards(): everything = lax.all_gather(quantized, 'row', axis=0, tiled=True)  12.8 us
    all_to_all x1, starting transfers between devices, fold_panels(): lax.all_to_all(jnp.stack([activations] * lax.axis_size('col')), 'col', 0, 0)  7.41 us
  transfers between devices with their start and end apart: 2, of which 0 were waited for; matrix products, arithmetic and copies ran while one was open for 71% of the time, Pallas kernels for 0%

profile of v1, /device:TPU:0, one launch (start us, length us, event | category | flops | bytes accessed | tf_op | source)
XLA Modules:
  0.0 125.2 jit_solution(5906629094561902594)
XLA Ops:
  7.2 1.9 %stack.2 = bf16[16,8,4096]{2,1,0:T(8,128)(2,1)} broadcast(bf16[8,4096]{1,0:T(8,128)(2,1)} %param.5), dimensions={1,2} | broadcast | bytes 1114112 | tf_op jit(solution)/shard_map/stack | solution.py:33
  9.1 7.4 %all-to-all-start = ((bf16[16,8,4096]{2,1,0:T(8,128)(2,1)}), bf16[16,8,4096]{2,1,0:T(8,128)(2,1)S(1)}, u32[]{:S(2)}, u32[]{:S(2)}) async-start(bf16[16,8,4096]{2,1,0:T(8,128)(2,1)} %stack.2), calls=%async_computation | async-start | bytes 2097152 | tf_op jit(solution)/shard_map/all_to_all | solution.py:33
  16.5 0.0 reduce-scatter.2.cloned.1.call-start
  17.2 1.6 %fusion.9 = bf16[64,3328]{1,0:T(8,128)(2,1)S(1)} fusion(bf16[64,3328]{1,0:T(8,128)(2,1)} %param.7, s32[]{:T(128)} %bitcast, s32[3328]{0:T(1024)S(1)} %iota_add_fusion, s32[64]{0:T(128)} %param.9), kind=kLoop, calls=%fused_computation.13 | loop fusion | flops 3833856 | bytes 865540 | tf_op jit(solution)/shard_map/convert_element_type | solution.py:16
  18.8 12.8 %all_gather.3 = bf16[128,3328]{1,0:T(8,128)(2,1)S(1)} all-gather(bf16[64,3328]{1,0:T(8,128)(2,1)S(1)} %fusion.9), channel_id=1, replica_groups=mesh['row'=2,'col'=16] {'row'}, dimensions={0}, use_global_device_ids=true | all-gather | bytes 1277952 | tf_op jit(solution)/shard_map/all_gather | solution.py:46
  31.6 15.0 %convolution_convert_fusion = bf16[128,4096]{1,0:T(8,128)(2,1)} fusion(bf16[128,3328]{1,0:T(8,128)(2,1)S(1)} %all_gather.3, bf16[4096,3328]{1,0:T(8,128)(2,1)} %param.6), kind=kOutput, calls=%fused_computation.1 | convolution fusion | flops 3490185216 | bytes 29163520 | tf_op jit(solution)/shard_map/dot_general | solution.py:26
  46.6 0.0 reduce-scatter.2.cloned.1.call-update
  46.6 0.0 all-to-all-done
  46.6 21.6 %multiply_bitcast_fusion = f32[4096,3328]{0,1:T(8,128)} fusion(bf16[128,3328]{1,0:T(8,128)(2,1)S(1)} %all_gather.3, bf16[16,8,4096]{2,1,0:T(8,128)(2,1)S(1)} %all-to-all-done), kind=kOutput, calls=%fused_computation | convolution fusion | flops 3503292416 | bytes 56426496 | tf_op jit(solution)/shard_map/dot_general | solution.py:20
  68.2 50.1 %copy.7 = f32[4096,3328]{1,0:T(8,128)} copy(f32[4096,3328]{0,1:T(8,128)} %multiply_bitcast_fusion) | data formatting | bytes 109051904
  118.3 0.0 reduce-scatter.2.cloned.1.call-done
  (1 shorter events, 0.0 us)
Async XLA Ops:
  9.1 37.5 %all-to-all-start = ((bf16[16,8,4096]{2,1,0:T(8,128)(2,1)}), bf16[16,8,4096]{2,1,0:T(8,128)(2,1)S(1)}, u32[]{:S(2)}, u32[]{:S(2)}) async-start(bf16[16,8,4096]{2,1,0:T(8,128)(2,1)} %stack.2), calls=%async_computation | async-start | bytes 2097152 | tf_op jit(solution)/shard_map/all_to_all | solution.py:33
  16.5 101.8 %reduce-scatter.2.cloned.1.call-start = ((), (), s32[]{:S(2)}) async-start(), calls=%async_computation.2 | async-start | bytes 1114112 | tf_op jit(solution)/shard_map/reduce_scatter | solution.py:52
Sparse Core Ops, SparseCore 0:
  46.7 58.5 reduce-scatter.1
